TPU v7x, 32 devices: a whole 2x2x4 slice. The times are simulated.
32 devices in a mesh: dp: 4 (over y, x), expert: 8 (over z, core).
Axes of the slice: x: 2, y: 2, z: 4, core: 2. Of those that a mesh axis runs over, the one named last changes fastest.
Arguments:
- tokens: bfloat16 [2, 32, 256, 1024], P(None, ('dp', 'expert')), may hold values from -6 to 6
- segment_ids: int32 [2, 32, 256], P(None, ('dp', 'expert')), may hold values from 0 to 15, never falling along the last dimension, each value on 1 to 128 neighbouring positions
- routes: int32 [2, 32, 256, 1], P(None, ('dp', 'expert')), may hold values from 0 to 7
- cotangent: bfloat16 [2, 32, 256, 1024], P(None, ('dp', 'expert')), may hold values from -6 to 6
- w_qkv: bfloat16 [1024, 3072], P(('dp', 'expert')), may hold values from -0.25 to 0.25
- w_attn_out: bfloat16 [1024, 1024], P(('dp', 'expert')), may hold values from -0.5 to 0.5
- w_router: bfloat16 [1024, 8], P(('dp', 'expert')), may hold values from -0.125 to 0.125
- gain_attn: bfloat16 [1024], P(('dp', 'expert')), may hold values from 0.099609375 to 1.8984375
- gain_moe: bfloat16 [1024], P(('dp', 'expert')), may hold values from 0.099609375 to 1.8984375
- w_expert_in: bfloat16 [8, 1024, 4096], P('expert', 'dp'), may hold values from -0.1875 to 0.1875
- w_expert_out: bfloat16 [8, 4096, 1024], P('expert', 'dp'), may hold values from -0.75 to 0.75
Outputs:
- output: bfloat16 [2, 32, 256, 1024], P(None, ('dp', 'expert'))
- grad_tokens: float32 [2, 32, 256, 1024], P(None, ('dp', 'expert'))
- grad_qkv: float32 [1024, 3072], P(('dp', 'expert'))
- grad_attn_out: float32 [1024, 1024], P(('dp', 'expert'))
- grad_router: float32 [1024, 8], P(('dp', 'expert'))
- grad_gain_attn: float32 [1024], P(('dp', 'expert'))
- grad_gain_moe: float32 [1024], P(('dp', 'expert'))
- grad_expert_in: float32 [8, 1024, 4096], P('expert', 'dp')
- grad_expert_out: float32 [8, 4096, 1024], P('expert', 'dp')
Inputs may be any that keep to these rules, and one draw needn't show every extreme that they name: `segment_ids`: in each sequence the numbers never fall; a document spans 1 to 128 positions, and in each sequence one spans exactly that many.
All inputs are finite; a program needn't handle non-finite values.
Results may differ from a plain program's by a relative error of at most 0.014.
The roundings to bfloat16 on the way count: a program that leaves them out, or rounds other values in their place, can miss the bound.
Values may be sent and summed in bfloat16 or wider, within the bound.
A program may use at most 256 MiB of HBM per device.

v0:
```python
import math
import jax
import jax.numpy as jnp
from jax import lax
from jax.sharding import PartitionSpec as P

HEADS = 16
epsilon = 1e-05
masked_value = -1e30


def normalize(values):
    row_mean = jnp.mean(values, axis=-1, keepdims=True)
    centered = values - row_mean
    inv_scale = lax.rsqrt(jnp.mean(centered * centered, axis=-1, keepdims=True) + epsilon)
    return (centered * inv_scale, inv_scale)


def norm_back(grad_normed, normed, inv_scale):
    return inv_scale * (
        grad_normed
        - jnp.mean(grad_normed, axis=-1, keepdims=True)
        - normed * jnp.mean(grad_normed * normed, axis=-1, keepdims=True)
    )


def fetch_attention(attn_local):
    return (
        lax.all_gather(attn_local[0], ("dp", "expert"), axis=0, tiled=True),
        lax.all_gather(attn_local[1], ("dp", "expert"), axis=0, tiled=True),
        lax.all_gather(attn_local[2], ("dp", "expert"), axis=0, tiled=True),
        lax.all_gather(attn_local[3], ("dp", "expert"), axis=0, tiled=True),
        lax.all_gather(attn_local[4], ("dp", "expert"), axis=0, tiled=True),
    )


def fetch_experts(expert_local):
    return (
        lax.all_gather(expert_local[0], "dp", axis=1, tiled=True),
        lax.all_gather(expert_local[1], "dp", axis=1, tiled=True),
    )


def score_block(query_rows, key_rows, allowed, score_scale):
    scores = (
        jnp.einsum("shd,thd->hst", query_rows, key_rows, preferred_element_type=jnp.float32)
        * score_scale
    )
    return jnp.where(allowed[None], scores, masked_value)


def split_heads(qkv_rows, model_width):
    seq_len = qkv_rows.shape[0]
    head_dim = model_width // HEADS
    query_rows = qkv_rows[:, :model_width].reshape(seq_len, HEADS, head_dim)
    key_rows = qkv_rows[:, model_width : 2 * model_width].reshape(seq_len, HEADS, head_dim)
    value_rows = qkv_rows[:, 2 * model_width :].reshape(seq_len, HEADS, head_dim)
    return (query_rows, key_rows, value_rows)


def route_selector(route_row, expert_count, capacity):
    one_hot = (route_row[:, None] == lax.iota(jnp.int32, expert_count)[None, :]).astype(jnp.int32)
    earlier = jnp.cumsum(one_hot, axis=0, dtype=jnp.int32) - one_hot
    position = jnp.sum(earlier * one_hot, axis=1, dtype=jnp.int32)
    slot_index = jnp.where(position < capacity, route_row * capacity + position, -1)
    columns = lax.iota(jnp.int32, expert_count * capacity)
    selector = (slot_index[:, None] == columns[None, :]).astype(jnp.bfloat16)
    return (one_hot.astype(jnp.float32), selector)


def layer_forward(inputs, segment_row, route_row, attn_full, expert_full, capacity):
    w_qkv, w_attn_out, w_router, gain_attn, gain_moe = attn_full
    seq_len, model_width = inputs.shape
    expert_count = w_router.shape[1]
    score_scale = 1.0 / math.sqrt(model_width // HEADS)
    normed_one, inv_one = normalize(inputs)
    attn_in = (normed_one * gain_attn.astype(jnp.float32)).astype(jnp.bfloat16)
    qkv_rows = jnp.dot(attn_in, w_qkv, preferred_element_type=jnp.float32).astype(jnp.bfloat16)
    query_rows, key_rows, value_rows = split_heads(qkv_rows, model_width)
    position = lax.iota(jnp.int32, seq_len)
    allowed = (position[None, :] <= position[:, None]) & (
        segment_row[:, None] == segment_row[None, :]
    )
    masked = score_block(query_rows, key_rows, allowed, score_scale)
    row_max = jnp.max(masked, axis=-1, keepdims=True)
    log_norm = row_max + jnp.log(jnp.sum(jnp.exp(masked - row_max), axis=-1, keepdims=True))
    attn_prob = jnp.exp(masked - log_norm).astype(jnp.bfloat16)
    attn_mixed = jnp.einsum(
        "hst,thd->shd", attn_prob, value_rows, preferred_element_type=jnp.float32
    )
    attn_mixed = attn_mixed.reshape(seq_len, model_width).astype(jnp.bfloat16)
    residual = inputs + jnp.dot(attn_mixed, w_attn_out, preferred_element_type=jnp.float32)
    normed_two, inv_two = normalize(residual)
    hidden_in = (normed_two * gain_moe.astype(jnp.float32)).astype(jnp.bfloat16)
    router_prob = jax.nn.softmax(
        jnp.dot(hidden_in, w_router, preferred_element_type=jnp.float32), axis=-1
    )
    one_hot, selector = route_selector(route_row, expert_count, capacity)
    gate_prob = jnp.sum(router_prob * one_hot, axis=1)
    buffer = jnp.einsum("sc,sd->cd", selector, hidden_in, preferred_element_type=jnp.float32)
    buffer = buffer.astype(jnp.bfloat16).reshape(expert_count, capacity, model_width)
    received = lax.all_to_all(buffer, "expert", split_axis=0, concat_axis=0, tiled=True).reshape(
        expert_count * capacity, model_width
    )
    pre_act = jnp.dot(received, expert_full[0][0], preferred_element_type=jnp.float32)
    activation = jax.nn.gelu(pre_act).astype(jnp.bfloat16)
    expert_rows = jnp.dot(activation, expert_full[1][0], preferred_element_type=jnp.float32)
    expert_rows = expert_rows.astype(jnp.bfloat16).reshape(expert_count, capacity, model_width)
    returned = lax.all_to_all(
        expert_rows, "expert", split_axis=0, concat_axis=0, tiled=True
    ).reshape(expert_count * capacity, model_width)
    moe_rows = jnp.einsum("sc,cd->sd", selector, returned, preferred_element_type=jnp.float32)
    output = residual + gate_prob[:, None] * moe_rows
    forward_state = (
        normed_one,
        inv_one,
        attn_in,
        qkv_rows,
        allowed,
        log_norm,
        attn_mixed,
        normed_two,
        inv_two,
        hidden_in,
        router_prob,
        one_hot,
        selector,
        gate_prob,
        received,
        pre_act,
        activation,
        moe_rows,
    )
    return (output, forward_state)


def layer_backward(grad_out, attn_full, expert_full, forward_state):
    (
        normed_one,
        inv_one,
        attn_in,
        qkv_rows,
        allowed,
        log_norm,
        attn_mixed,
        normed_two,
        inv_two,
        hidden_in,
        router_prob,
        one_hot,
        selector,
        gate_prob,
        received,
        pre_act,
        activation,
        moe_rows,
    ) = forward_state
    w_qkv, w_attn_out, w_router, gain_attn, gain_moe = attn_full
    w_in = expert_full[0][0]
    w_out = expert_full[1][0]
    seq_len, model_width = grad_out.shape
    expert_count = w_router.shape[1]
    capacity = selector.shape[1] // expert_count
    score_scale = 1.0 / math.sqrt(model_width // HEADS)
    grad_gate = jnp.sum(grad_out * moe_rows, axis=1)
    grad_moe = (gate_prob[:, None] * grad_out).astype(jnp.bfloat16)
    grad_buffer = jnp.einsum("sc,sd->cd", selector, grad_moe, preferred_element_type=jnp.float32)
    grad_buffer = grad_buffer.astype(jnp.bfloat16).reshape(expert_count, capacity, model_width)
    grad_rows = lax.all_to_all(
        grad_buffer, "expert", split_axis=0, concat_axis=0, tiled=True
    ).reshape(expert_count * capacity, model_width)
    grad_activation = jnp.einsum("rd,fd->rf", grad_rows, w_out, preferred_element_type=jnp.float32)
    term_out = jnp.einsum("rf,rd->fd", activation, grad_rows, preferred_element_type=jnp.float32)
    gelu_slope = jax.vjp(jax.nn.gelu, pre_act)[1]
    grad_pre = gelu_slope(grad_activation)[0].astype(jnp.bfloat16)
    term_in = jnp.einsum("rd,rf->df", received, grad_pre, preferred_element_type=jnp.float32)
    grad_received = jnp.einsum("rf,df->rd", grad_pre, w_in, preferred_element_type=jnp.float32)
    grad_received = grad_received.astype(jnp.bfloat16).reshape(expert_count, capacity, model_width)
    grad_back = lax.all_to_all(
        grad_received, "expert", split_axis=0, concat_axis=0, tiled=True
    ).reshape(expert_count * capacity, model_width)
    grad_hidden = jnp.einsum("sc,cd->sd", selector, grad_back, preferred_element_type=jnp.float32)
    grad_choice = one_hot * grad_gate[:, None]
    grad_logit = router_prob * (
        grad_choice - jnp.sum(router_prob * grad_choice, axis=1, keepdims=True)
    )
    grad_logit = grad_logit.astype(jnp.bfloat16)
    term_router = jnp.einsum("sd,se->de", hidden_in, grad_logit, preferred_element_type=jnp.float32)
    grad_hidden = grad_hidden + jnp.einsum(
        "se,de->sd", grad_logit, w_router, preferred_element_type=jnp.float32
    )
    term_gain_moe = jnp.sum(grad_hidden * normed_two, axis=0)
    grad_resid = grad_out + norm_back(
        grad_hidden * gain_moe.astype(jnp.float32), normed_two, inv_two
    )
    grad_branch = grad_resid.astype(jnp.bfloat16)
    term_attn_out = jnp.einsum(
        "sd,se->de", attn_mixed, grad_branch, preferred_element_type=jnp.float32
    )
    grad_mixed = jnp.einsum(
        "se,de->sd", grad_branch, w_attn_out, preferred_element_type=jnp.float32
    )
    grad_mixed = grad_mixed.astype(jnp.bfloat16).reshape(seq_len, HEADS, model_width // HEADS)
    query_rows, key_rows, value_rows = split_heads(qkv_rows, model_width)
    masked = score_block(query_rows, key_rows, allowed, score_scale)
    attn_prob = jnp.exp(masked - log_norm)
    grad_prob = jnp.einsum(
        "shd,thd->hst", grad_mixed, value_rows, preferred_element_type=jnp.float32
    )
    grad_value = jnp.einsum(
        "hst,shd->thd",
        attn_prob.astype(jnp.bfloat16),
        grad_mixed,
        preferred_element_type=jnp.float32,
    )
    grad_score = attn_prob * (grad_prob - jnp.sum(attn_prob * grad_prob, axis=-1, keepdims=True))
    grad_score = grad_score.astype(jnp.bfloat16)
    grad_query = (
        jnp.einsum("hst,thd->shd", grad_score, key_rows, preferred_element_type=jnp.float32)
        * score_scale
    )
    grad_key = (
        jnp.einsum("hst,shd->thd", grad_score, query_rows, preferred_element_type=jnp.float32)
        * score_scale
    )
    grad_qkv_rows = jnp.concatenate(
        [
            grad_query.reshape(seq_len, model_width),
            grad_key.reshape(seq_len, model_width),
            grad_value.reshape(seq_len, model_width),
        ],
        axis=1,
    ).astype(jnp.bfloat16)
    term_qkv = jnp.einsum("sd,sf->df", attn_in, grad_qkv_rows, preferred_element_type=jnp.float32)
    grad_attn_in = jnp.einsum("sf,df->sd", grad_qkv_rows, w_qkv, preferred_element_type=jnp.float32)
    term_gain_attn = jnp.sum(grad_attn_in * normed_one, axis=0)
    grad_inputs = grad_resid + norm_back(
        grad_attn_in * gain_attn.astype(jnp.float32), normed_one, inv_one
    )
    attn_terms = (term_qkv, term_attn_out, term_router, term_gain_attn, term_gain_moe)
    expert_terms = (term_in[None], term_out[None])
    return (grad_inputs, attn_terms, expert_terms)


def on_device(
    tokens,
    segment_ids,
    routes,
    cotangent,
    w_qkv,
    w_attn_out,
    w_router,
    gain_attn,
    gain_moe,
    w_expert_in,
    w_expert_out,
):
    micro_count = tokens.shape[0]
    seq_len = tokens.shape[2]
    expert_count = w_router.shape[1]
    capacity = (9 * seq_len + 8 * expert_count - 1) // (8 * expert_count)
    attn_local = (w_qkv, w_attn_out, w_router, gain_attn, gain_moe)
    expert_local = (w_expert_in, w_expert_out)
    attn_total = None
    expert_total = None
    outputs = []
    grads_in = []
    for micro_idx in range(micro_count):
        attn_full = fetch_attention(attn_local)
        expert_full = fetch_experts(expert_local)
        inputs = tokens[micro_idx, 0].astype(jnp.float32)
        output, forward_state = layer_forward(
            inputs,
            segment_ids[micro_idx, 0],
            routes[micro_idx, 0, :, 0],
            attn_full,
            expert_full,
            capacity,
        )
        outputs.append(output.astype(jnp.bfloat16))
        attn_full = fetch_attention(attn_local)
        expert_full = fetch_experts(expert_local)
        grad_inputs, attn_terms, expert_terms = layer_backward(
            cotangent[micro_idx, 0].astype(jnp.float32), attn_full, expert_full, forward_state
        )
        grads_in.append(grad_inputs)
        attn_total = (
            attn_terms if attn_total is None else jax.tree.map(jnp.add, attn_total, attn_terms)
        )
        expert_total = (
            expert_terms
            if expert_total is None
            else jax.tree.map(jnp.add, expert_total, expert_terms)
        )
    attn_total = (
        lax.psum_scatter(attn_total[0], ("dp", "expert"), scatter_dimension=0, tiled=True),
        lax.psum_scatter(attn_total[1], ("dp", "expert"), scatter_dimension=0, tiled=True),
        lax.psum_scatter(attn_total[2], ("dp", "expert"), scatter_dimension=0, tiled=True),
        lax.psum_scatter(attn_total[3], ("dp", "expert"), scatter_dimension=0, tiled=True),
        lax.psum_scatter(attn_total[4], ("dp", "expert"), scatter_dimension=0, tiled=True),
    )
    expert_total = (
        lax.psum_scatter(
            expert_total[0].astype(jnp.bfloat16), "dp", scatter_dimension=1, tiled=True
        ).astype(jnp.float32),
        lax.psum_scatter(
            expert_total[1].astype(jnp.bfloat16), "dp", scatter_dimension=1, tiled=True
        ).astype(jnp.float32),
    )
    output_all = jnp.stack(outputs)[:, None]
    grad_tokens = jnp.stack(grads_in)[:, None]
    return (
        output_all,
        grad_tokens,
        attn_total[0],
        attn_total[1],
        attn_total[2],
        attn_total[3],
        attn_total[4],
        expert_total[0],
        expert_total[1],
    )


def solution(mesh):
    in_specs = (
        P(None, ("dp", "expert"), None, None),
        P(None, ("dp", "expert"), None),
        P(None, ("dp", "expert"), None, None),
        P(None, ("dp", "expert"), None, None),
        P(("dp", "expert"), None),
        P(("dp", "expert"), None),
        P(("dp", "expert"), None),
        P(("dp", "expert")),
        P(("dp", "expert")),
        P("expert", "dp", None),
        P("expert", "dp", None),
    )
    out_specs = (
        P(None, ("dp", "expert"), None, None),
        P(None, ("dp", "expert"), None, None),
        P(("dp", "expert"), None),
        P(("dp", "expert"), None),
        P(("dp", "expert"), None),
        P(("dp", "expert")),
        P(("dp", "expert")),
        P("expert", "dp", None),
        P("expert", "dp", None),
    )
    return jax.shard_map(
        on_device, mesh=mesh, in_specs=in_specs, out_specs=out_specs, check_vma=False
    )
```

profile of v0, /device:TPU:0, one launch (start us, length us, event | category | flops | bytes accessed | tf_op | source)
XLA Modules:
  0.0 1070.3 jit_solution(837478429790069913)
XLA Ops:
  10.5 42.6 %all-reduce.5 = (bf16[1024]{0:T(1024)(128)(2,1)S(1)}, bf16[1024]{0:T(1024)(128)(2,1)S(1)}) all-reduce(bf16[1024]{0:T(1024)(128)(2,1)S(1)} %dynamic-update-slice, bf16[1024]{0:T(1024)(128)(2,1)S(1)} %dynamic-update-slice.1), channel_id=1, replica_groups=mesh['dp'=4,'expert'=8] {'dp','expert'}, use_global_device_ids=true, to_apply=%add | all-reduce | flops 2048 | bytes 8192
  55.1 28.3 %all-gather.6.cloned.1.call-done = bf16[1024,3072]{1,0:T(8,128)(2,1)} async-done(((bf16[32,3072]{1,0:T(8,128)(2,1)}), bf16[1024,3072]{1,0:T(8,128)(2,1)}) %all-gather.6.cloned.1.call-update) | async-done | bytes 6291472 | tf_op jit(solution)/shard_map/all_gather | solution.py:29
  83.4 4.7 convolution_convert_fusion
  90.6 4.7 convolution_convert_fusion.1
  102.8 38.5 %all-gather.8.cloned.1.call-done = bf16[1024,1024]{1,0:T(8,128)(2,1)} async-done(((bf16[32,1024]{1,0:T(8,128)(2,1)}), bf16[1024,1024]{1,0:T(8,128)(2,1)}) %all-gather.8.cloned.1.call-update) | async-done | bytes 2097168 | tf_op jit(solution)/shard_map/all_gather | solution.py:30
  159.8 13.8 %all-to-all-done.2 = bf16[8,36,1024]{2,1,0:T(8,128)(2,1)S(1)} async-done(((bf16[8,36,1024]{2,1,0:T(8,128)(2,1)}), bf16[8,36,1024]{2,1,0:T(8,128)(2,1)S(1)}, u32[]{:S(2)}, u32[]{:S(2)}) %all-to-all-start.2) | async-done | bytes 589856 | tf_op jit(solution)/shard_map/all_to_all | solution.py:102
  178.8 50.8 %all-gather.10.cloned.1.call-done = bf16[1,1024,4096]{2,1,0:T(8,128)(2,1)} async-done(((bf16[1,256,4096]{2,1,0:T(8,128)(2,1)}), bf16[1,1024,4096]{2,1,0:T(8,128)(2,1)}) %all-gather.10.cloned.1.call-update) | async-done | bytes 8388624 | tf_op jit(solution)/shard_map/all_gather | solution.py:39
  229.5 8.3 fusion.14
  237.8 80.9 %all-gather.12.cloned.1.call-done = bf16[1,4096,1024]{2,1,0:T(8,128)(2,1)} async-done(((bf16[1,1024,1024]{2,1,0:T(8,128)(2,1)}), bf16[1,4096,1024]{2,1,0:T(8,128)(2,1)}) %all-gather.12.cloned.1.call-update) | async-done | bytes 8388624 | tf_op jit(solution)/shard_map/all_gather | solution.py:40
  318.8 7.8 fusion.49
  333.4 5.2 fusion.16
  340.8 7.3 fusion.46
  350.4 4.8 all-to-all-start.1
  355.2 47.5 %all-gather = bf16[32,32,8]{1,2,0:T(8,128)(2,1)S(1)} all-gather(bf16[1,32,8]{1,2,0:T(8,128)(2,1)S(1)} %bitcast.292), channel_id=1, replica_groups=mesh['dp'=4,'expert'=8] {'dp','expert'}, dimensions={0}, use_global_device_ids=true | all-gather | bytes 16896 | tf_op jit(solution)/shard_map/all_gather | solution.py:31
  424.6 14.2 %all-to-all-done.4 = bf16[8,36,1024]{2,1,0:T(8,128)(2,1)} async-done(((bf16[8,36,1024]{2,1,0:T(8,128)(2,1)}), bf16[8,36,1024]{2,1,0:T(8,128)(2,1)}, u32[]{:S(2)}, u32[]{:S(2)}) %all-to-all-start.4) | async-done | bytes 589856 | tf_op jit(solution)/shard_map/all_to_all | solution.py:169
  446.9 13.2 %fusion.177 = f32[4096,1024]{1,0:T(8,128)} fusion(bf16[288,1024]{1,0:T(8,128)(2,1)} %reshape.406, f32[288,4096]{1,0:T(8,128)} %copy-done.15), kind=kOutput, calls=%fused_computation.253 | convolution fusion | flops 2426535936 | bytes 22085632 | tf_op jit(solution)/shard_map/rf,rd->fd/dot_general | solution.py:173
  461.7 15.6 %fusion.1 = bf16[1,4096,1024]{2,1,0:T(8,128)(2,1)} fusion(f32[4096,1024]{1,0:T(8,128)} %fusion.177, bf16[288,1024]{1,0:T(8,128)(2,1)} %reshape.414, f32[288,4096]{1,0:T(8,128)} %fusion.14), kind=kOutput, calls=%fused_computation.3 | convolution fusion | flops 2434924544 | bytes 30474240 | tf_op jit(solution)/shard_map/rf,rd->fd/dot_general | solution.py:173
  478.3 11.6 %fusion.24 = bf16[288,4096]{1,0:T(8,128)(2,1)S(1)} fusion(f32[288,4096]{1,0:T(8,128)} %copy-done.15, bf16[288,1024]{1,0:T(8,128)(2,1)S(1)} %copy-done.28, bf16[1,4096,1024]{2,1,0:T(8,128)(2,1)} %all-gather.12.cloned.1.call-done), kind=kOutput, calls=%fused_computation.31 | convolution fusion | flops 2439512064 | bytes 16056320 | tf_op jit(solution)/shard_map/rd,fd->rf/dot_general | solution.py:172
  490.0 8.1 fusion.186
  498.1 11.7 %fusion.31 = bf16[288,4096]{1,0:T(8,128)(2,1)S(1)} fusion(f32[288,4096]{1,0:T(8,128)} %fusion.14, bf16[288,1024]{1,0:T(8,128)(2,1)S(1)} %copy-done.30, bf16[1,4096,1024]{2,1,0:T(8,128)(2,1)} %all-gather.12.cloned.1.call-done), kind=kOutput, calls=%fused_computation.38 | convolution fusion | flops 2439512064 | bytes 16056320 | tf_op jit(solution)/shard_map/rd,fd->rf/dot_general | solution.py:172
  511.2 10.3 fusion
  521.5 6.8 fusion.40
  533.6 6.7 fusion.43
  541.3 11.1 %all-to-all-done.5 = bf16[8,36,1024]{2,1,0:T(8,128)(2,1)S(1)} async-done(((bf16[8,36,1024]{2,1,0:T(8,128)(2,1)}), bf16[8,36,1024]{2,1,0:T(8,128)(2,1)S(1)}, u32[]{:S(2)}, u32[]{:S(2)}) %all-to-all-start.5) | async-done | bytes 589856 | tf_op jit(solution)/shard_map/all_to_all | solution.py:179
  556.9 17.4 %all-to-all-done.7 = bf16[8,36,1024]{2,1,0:T(8,128)(2,1)S(1)} async-done(((bf16[8,36,1024]{2,1,0:T(8,128)(2,1)}), bf16[8,36,1024]{2,1,0:T(8,128)(2,1)S(1)}, u32[]{:S(2)}, u32[]{:S(2)}) %all-to-all-start.7) | async-done | bytes 589856 | tf_op jit(solution)/shard_map/all_to_all | solution.py:179
  610.5 6.8 convolution_add_fusion
  618.8 5.2 fusion.90
  624.0 6.8 fusion.84
  630.9 37.4 %all-reduce.4 = (f32[1024]{0:T(1024)S(1)}, f32[1024]{0:T(1024)S(1)}) all-reduce(f32[1024]{0:T(1024)S(1)} %add.172, f32[1024]{0:T(1024)S(1)} %add.173), channel_id=5, replica_groups=mesh['dp'=4,'expert'=8] {'dp','expert'}, use_global_device_ids=true, to_apply=%region_43.44.clone | all-reduce | flops 2048 | bytes 16384
  679.7 78.5 %reduce-scatter.12.cloned.1.call-done = bf16[1,256,4096]{2,1,0:T(8,128)(2,1)} async-done(((bf16[1,1024,4096]{2,1,0:T(8,128)(2,1)}), bf16[1,256,4096]{2,1,0:T(8,128)(2,1)}) %reduce-scatter.12.cloned.1.call-update) | async-done | bytes 2097168 | tf_op jit(solution)/shard_map/reduce_scatter | solution.py:303
  762.2 142.7 %reduce-scatter.10.cloned.1.call-done = f32[32,1024]{1,0:T(8,128)} async-done(((f32[1024,1024]{1,0:T(8,128)}), f32[32,1024]{1,0:T(8,128)}) %reduce-scatter.10.cloned.1.call-update) | async-done | bytes 131088 | tf_op jit(solution)/shard_map/reduce_scatter | solution.py:297
  904.9 158.4 %reduce-scatter.8.cloned.1.call-done = f32[32,3072]{1,0:T(8,128)} async-done(((f32[1024,3072]{1,0:T(8,128)}), f32[32,3072]{1,0:T(8,128)}) %reduce-scatter.8.cloned.1.call-update) | async-done | bytes 393232 | tf_op jit(solution)/shard_map/reduce_scatter | solution.py:296
  (300 shorter events, 146.9 us)
Async XLA Ops:
  7.2 45.9 %copy-start.66 = (s32[2,1,256,1]{2,3,1,0:T(1,128)S(1)}, s32[2,1,256,1]{2,3,1,0:T(1,128)}, u32[]{:S(2)}) copy-start(s32[2,1,256,1]{2,3,1,0:T(1,128)} %param.13) | copy-start | bytes 6148
  7.2 46.9 %copy-start.6 = (bf16[2,1,256,1024]{3,2,1,0:T(8,128)(2,1)S(1)}, bf16[2,1,256,1024]{3,2,1,0:T(8,128)(2,1)}, u32[]{:S(2)}) copy-start(bf16[2,1,256,1024]{3,2,1,0:T(8,128)(2,1)} %param.11) | copy-start | bytes 3145732
  7.2 47.6 %copy-start.67 = (s32[2,1,256]{2,1,0:T(1,128)S(1)}, s32[2,1,256]{2,1,0:T(1,128)}, u32[]{:S(2)}) copy-start(s32[2,1,256]{2,1,0:T(1,128)} %param.12) | copy-start | bytes 6148
  7.2 76.2 %all-gather.6.cloned.1.call-start = ((), (), s32[]{:S(2)}) async-start(), calls=%async_computation.13 | async-start | bytes 6488064 | tf_op jit(solution)/shard_map/all_gather | solution.py:29
  8.0 133.4 %all-gather.8.cloned.1.call-start = ((), (), s32[]{:S(2)}) async-start(), calls=%async_computation.14 | async-start | bytes 2162688 | tf_op jit(solution)/shard_map/all_gather | solution.py:30
  8.7 220.8 %all-gather.10.cloned.1.call-start = ((), (), s32[]{:S(2)}) async-start(), calls=%async_computation.15 | async-start | bytes 10485760 | tf_op jit(solution)/shard_map/all_gather | solution.py:39
  9.4 309.3 %all-gather.12.cloned.1.call-start = ((), (), s32[]{:S(2)}) async-start(), calls=%async_computation.16 | async-start | bytes 10485760 | tf_op jit(solution)/shard_map/all_gather | solution.py:40
  53.1 37.4 %copy-start.47 = (f32[1024]{0:T(1024)}, f32[1024]{0:T(1024)S(1)}, u32[]{:S(2)}) copy-start(f32[1024]{0:T(1024)S(1)} %convert_element_type.196) | copy-start | bytes 12292
  54.3 33.8 %copy-start.59 = (f32[256]{0:T(256)}, f32[256]{0:T(256)S(1)}, u32[]{:S(2)}) copy-start(f32[256]{0:T(256)S(1)} %get-tuple-element.104) | copy-start | bytes 3076
  54.3 36.2 %copy-start.57 = (f32[256]{0:T(256)}, f32[256]{0:T(256)S(1)}, u32[]{:S(2)}) copy-start(f32[256]{0:T(256)S(1)} %get-tuple-element.105) | copy-start | bytes 3076
  54.8 35.8 %copy-start.61 = (f32[256]{0:T(256)}, f32[256]{0:T(256)S(1)}, u32[]{:S(2)}) copy-start(f32[256]{0:T(256)S(1)} %add_rsqrt_fusion.3) | copy-start | bytes 3076
  54.8 33.3 %copy-start.63 = (f32[256]{0:T(256)}, f32[256]{0:T(256)S(1)}, u32[]{:S(2)}) copy-start(f32[256]{0:T(256)S(1)} %add_rsqrt_fusion.1) | copy-start | bytes 3076
  54.9 91.0 %copy-start.42 = (pred[256,256]{0,1:T(8,128)(4,1)}, pred[256,256]{0,1:T(8,128)(4,1)S(1)}, u32[]{:S(2)}) copy-start(pred[256,256]{0,1:T(8,128)(4,1)S(1)} %fusion.112) | copy-start | bytes 196612
  55.1 44.8 %copy-start.44 = (pred[256,256]{0,1:T(8,128)(4,1)}, pred[256,256]{0,1:T(8,128)(4,1)S(1)}, u32[]{:S(2)}) copy-start(pred[256,256]{0,1:T(8,128)(4,1)S(1)} %fusion.113) | copy-start | bytes 196612
  88.5 55.7 %copy-start.16 = (bf16[256,1024]{0,1:T(8,128)(2,1)}, bf16[256,1024]{0,1:T(8,128)(2,1)S(1)}, u32[]{:S(2)}) copy-start(bf16[256,1024]{0,1:T(8,128)(2,1)S(1)} %copy.72) | copy-start | bytes 1572868
  100.9 43.3 %copy-start.20 = (bf16[256,1024]{0,1:T(8,128)(2,1)S(1)}, bf16[256,1024]{0,1:T(8,128)(2,1)}, u32[]{:S(2)}) copy-start(bf16[256,1024]{0,1:T(8,128)(2,1)} %copy.71) | copy-start | bytes 1572868
  149.9 253.0 %copy-start.14 = (bf16[256,1024]{1,0:T(8,128)(2,1)}, bf16[256,1024]{1,0:T(8,128)(2,1)S(1)}, u32[]{:S(2)}) copy-start(bf16[256,1024]{1,0:T(8,128)(2,1)S(1)} %get-tuple-element.79) | copy-start | bytes 1572868
  152.0 21.6 %all-to-all-start.2 = ((bf16[8,36,1024]{2,1,0:T(8,128)(2,1)}), bf16[8,36,1024]{2,1,0:T(8,128)(2,1)S(1)}, u32[]{:S(2)}, u32[]{:S(2)}) async-start(bf16[8,36,1024]{2,1,0:T(8,128)(2,1)} %reshape.401), calls=%async_computation.2 | async-start | bytes 1310720 | tf_op jit(solution)/shard_map/all_to_all | solution.py:102
  173.7 153.9 %all-to-all-start = ((bf16[8,36,1024]{2,1,0:T(8,128)(2,1)}), bf16[8,36,1024]{2,1,0:T(8,128)(2,1)}, u32[]{:S(2)}, u32[]{:S(2)}) async-start(bf16[8,36,1024]{2,1,0:T(8,128)(2,1)} %reshape.393), calls=%async_computation | async-start | bytes 1310720 | tf_op jit(solution)/shard_map/all_to_all | solution.py:102
  327.6 22.9 %all-to-all-start.3 = ((bf16[8,36,1024]{2,1,0:T(8,128)(2,1)}), bf16[8,36,1024]{2,1,0:T(8,128)(2,1)}, u32[]{:S(2)}, u32[]{:S(2)}) async-start(bf16[8,36,1024]{2,1,0:T(8,128)(2,1)} %reshape.403), calls=%async_computation.3 | async-start | bytes 1310720 | tf_op jit(solution)/shard_map/all_to_all | solution.py:109
  350.4 56.3 %all-to-all-start.1 = ((bf16[8,36,1024]{2,1,0:T(8,128)(2,1)}), bf16[8,36,1024]{2,1,0:T(8,128)(2,1)}, u32[]{:S(2)}, u32[]{:S(2)}) async-start(bf16[8,36,1024]{2,1,0:T(8,128)(2,1)} %reshape.395), calls=%async_computation.1 | async-start | bytes 1310720 | tf_op jit(solution)/shard_map/all_to_all | solution.py:109
  416.5 22.3 %all-to-all-start.4 = ((bf16[8,36,1024]{2,1,0:T(8,128)(2,1)}), bf16[8,36,1024]{2,1,0:T(8,128)(2,1)}, u32[]{:S(2)}, u32[]{:S(2)}) async-start(bf16[8,36,1024]{2,1,0:T(8,128)(2,1)} %reshape.405), calls=%async_computation.4 | async-start | bytes 1310720 | tf_op jit(solution)/shard_map/all_to_all | solution.py:169
  422.0 21.6 %copy-start.13 = (bf16[256,1024]{1,0:T(8,128)(2,1)S(1)}, bf16[256,1024]{1,0:T(8,128)(2,1)}, u32[]{:S(2)}) copy-start(bf16[256,1024]{1,0:T(8,128)(2,1)} %copy-done.12) | copy-start | bytes 1572868
  438.8 22.0 %all-to-all-start.6 = ((bf16[8,36,1024]{2,1,0:T(8,128)(2,1)}), bf16[8,36,1024]{2,1,0:T(8,128)(2,1)S(1)}, u32[]{:S(2)}, u32[]{:S(2)}) async-start(bf16[8,36,1024]{2,1,0:T(8,128)(2,1)} %reshape.413), calls=%async_computation.6 | async-start | bytes 1310720 | tf_op jit(solution)/shard_map/all_to_all | solution.py:169
  442.3 175.1 %reduce-scatter.16.cloned.1.call-start = ((), (), s32[]{:S(2)}) async-start(), calls=%async_computation.21 | async-start | bytes 540672
  444.9 230.7 %reduce-scatter.14.cloned.1.call-start = ((), (), s32[]{:S(2)}) async-start(), calls=%async_computation.20 | async-start | bytes 10485760 | tf_op jit(solution)/shard_map/reduce_scatter | solution.py:306
  477.3 280.8 %reduce-scatter.12.cloned.1.call-start = ((), (), s32[]{:S(2)}) async-start(), calls=%async_computation.19 | async-start | bytes 10485760 | tf_op jit(solution)/shard_map/reduce_scatter | solution.py:303
  529.2 23.1 %all-to-all-start.5 = ((bf16[8,36,1024]{2,1,0:T(8,128)(2,1)}), bf16[8,36,1024]{2,1,0:T(8,128)(2,1)S(1)}, u32[]{:S(2)}, u32[]{:S(2)}) async-start(bf16[8,36,1024]{2,1,0:T(8,128)(2,1)} %reshape.407), calls=%async_computation.5 | async-start | bytes 1310720 | tf_op jit(solution)/shard_map/all_to_all | solution.py:179
  552.4 22.0 %all-to-all-start.7 = ((bf16[8,36,1024]{2,1,0:T(8,128)(2,1)}), bf16[8,36,1024]{2,1,0:T(8,128)(2,1)S(1)}, u32[]{:S(2)}, u32[]{:S(2)}) async-start(bf16[8,36,1024]{2,1,0:T(8,128)(2,1)} %reshape.415), calls=%async_computation.7 | async-start | bytes 1310720 | tf_op jit(solution)/shard_map/all_to_all | solution.py:179
  555.9 349.0 %reduce-scatter.10.cloned.1.call-start = ((), (), s32[]{:S(2)}) async-start(), calls=%async_computation.18 | async-start | bytes 4325376 | tf_op jit(solution)/shard_map/reduce_scatter | solution.py:297
  584.2 479.0 %reduce-scatter.8.cloned.1.call-start = ((), (), s32[]{:S(2)}) async-start(), calls=%async_computation.17 | async-start | bytes 12976128 | tf_op jit(solution)/shard_map/reduce_scatter | solution.py:296
  624.0 47.7 %copy-start.9 = (f32[256,1024]{1,0:T(8,128)S(1)}, f32[256,1024]{1,0:T(8,128)}, u32[]{:S(2)}) copy-start(f32[256,1024]{1,0:T(8,128)} %copy-done.8) | copy-start | bytes 3145732
  (56 other events, 211.6 us)
Sparse Core Ops, SparseCore 0:
  11.0 72.3 all-gather.5
  86.4 54.8 all-gather.7
  143.2 86.3 all-gather.9
  231.2 87.4 all-gather.11
  445.1 136.7 reduce-scatter.15
  584.8 83.8 reduce-scatter.13
  671.8 86.3 reduce-scatter.11
  761.0 143.8 reduce-scatter.9
  911.5 151.7 reduce-scatter.7
where the time goes:
time: 1080 us; the launch traced here: 1070 us
  waiting for transfers between devices  638 us (59%)
  matrix products  186 us (17%)
  blocking collectives  128 us (12%)
  local copies, waits for them, and re-layouts  45.5 us (4%)
  starting transfers between devices  33.8 us (3%)
  other arithmetic  23.6 us (2%)
  between operations  15.6 us (1%)
    reduce_scatter x1, waiting for transfers between devices, on_device(): lax.psum_scatter(attn_total[0], ('dp', 'expert'), scatter_dimension=0, ti...  158 us
    reduce_scatter x1, waiting for transfers between devices, on_device(): lax.psum_scatter(attn_total[1], ('dp', 'expert'), scatter_dimension=0, ti...  143 us
    all_gather x1, waiting for transfers between devices, fetch_experts(): lax.all_gather(expert_local[1], 'dp', axis=1, tiled=True)  80.9 us
    unnamed x2, blocking collectives  80 us
    reduce_scatter x1, waiting for transfers between devices, on_device(): lax.psum_scatter(expert_total[0].astype(jnp.bfloat16), 'dp', scatter_dime...  78.5 us
    all_gather x1, waiting for transfers between devices, fetch_experts(): lax.all_gather(expert_local[0], 'dp', axis=1, tiled=True)  50.8 us
    all_gather x1, blocking collectives, fetch_attention(): lax.all_gather(attn_local[2], ('dp', 'expert'), axis=0, tiled=True)  47.5 us
    all_gather x1, waiting for transfers between devices, fetch_attention(): lax.all_gather(attn_local[1], ('dp', 'expert'), axis=0, tiled=True)  38.5 us
  transfers between devices with their start and end apart: 17, of which 13 were waited for; matrix products, arithmetic and copies ran while one was open for 22% of the time, Pallas kernels for 0%

commit v1 on v0

--- a/solution.py
+++ b/solution.py
@@ -27,7 +27,12 @@
 def fetch_attention(attn_local):
     return (
         lax.all_gather(attn_local[0], ("dp", "expert"), axis=0, tiled=True),
-        lax.all_gather(attn_local[1], ("dp", "expert"), axis=0, tiled=True),
+        jnp.concatenate(
+            lax.all_to_all(
+                jnp.stack([attn_local[1]] * lax.axis_size(("dp", "expert"))), ("dp", "expert"), 0, 0
+            ),
+            axis=0,
+        ),
         lax.all_gather(attn_local[2], ("dp", "expert"), axis=0, tiled=True),
         lax.all_gather(attn_local[3], ("dp", "expert"), axis=0, tiled=True),
         lax.all_gather(attn_local[4], ("dp", "expert"), axis=0, tiled=True),

time: 1080 us -> 1030 us (0.954)
  waiting for transfers between devices: 638 us -> 549 us
  blocking collectives: 128 us -> 173 us
    unnamed x2, blocking collectives: 80 us -> 125 us
    all_gather x1 -> x0, waiting for transfers between devices: 38.5 us -> none  [fetch_attention(): lax.all_gather(attn_local[1], ('dp', 'expert'), axis=0, tiled=True)]
    all_gather x1, waiting for transfers between devices: 50.8 us -> 13.9 us  [fetch_experts(): lax.all_gather(expert_local[0], 'dp', axis=1, tiled=True)]
    all_gather x1, waiting for transfers between devices: 28.3 us -> 0.02 us  [fetch_attention(): lax.all_gather(attn_local[0], ('dp', 'expert'), axis=0, tiled=True)]
  transfers between devices with their start and end apart: 17 -> 17, of which waited for: 13 -> 11; matrix products, arithmetic and copies ran while one was open for 22% -> 23% of each run, Pallas kernels for 0% -> 0%
where the time goes in v1:
time: 1030 us; the launch traced here: 1020 us
  waiting for transfers between devices  549 us (53%)
  matrix products  176 us (17%)
  blocking collectives  173 us (17%)
  local copies, waits for them, and re-layouts  46.6 us (5%)
  starting transfers between devices  38.2 us (4%)
  other arithmetic  24.1 us (2%)
  between operations  15.7 us (2%)
    reduce_scatter x1, waiting for transfers between devices, on_device(): lax.psum_scatter(attn_total[0], ('dp', 'expert'), scatter_dimension=0, ti...  159 us
    reduce_scatter x1, waiting for transfers between devices, on_device(): lax.psum_scatter(attn_total[1], ('dp', 'expert'), scatter_dimension=0, ti...  143 us
    unnamed x2, blocking collectives  125 us
    all_gather x1, waiting for transfers between devices, fetch_experts(): lax.all_gather(expert_local[1], 'dp', axis=1, tiled=True)  81.8 us
    reduce_scatter x1, waiting for transfers between devices, on_device(): lax.psum_scatter(expert_total[0].astype(jnp.bfloat16), 'dp', scatter_dime...  80.8 us
    all_gather x1, blocking collectives, fetch_attention(): lax.all_gather(attn_local[2], ('dp', 'expert'), axis=0, tiled=True)  47.4 us
    all_to_all x2, waiting for transfers between devices, layer_backward(): lax.all_to_all(grad_received, 'expert', split_axis=0, concat_axis=0, tile...  28.8 us
    dot_general x2, matrix products, layer_backward(): jnp.einsum('rf,rd->fd', activation, grad_rows, preferred_element_type=jnp...  23.6 us
  transfers between devices with their start and end apart: 17, of which 11 were waited for; matrix products, arithmetic and copies ran while one was open for 23% of the time, Pallas kernels for 0%

profile of v1, /device:TPU:0, one launch (start us, length us, event | category | flops | bytes accessed | tf_op | source)
XLA Modules:
  0.0 1022.3 jit_solution(9056450220116369389)
XLA Ops:
  11.0 7.3 all-to-all-start
  20.4 87.6 %all-reduce.5 = (bf16[1024]{0:T(1024)(128)(2,1)S(1)}, bf16[1024]{0:T(1024)(128)(2,1)S(1)}) all-reduce(bf16[1024]{0:T(1024)(128)(2,1)S(1)} %dynamic-update-slice, bf16[1024]{0:T(1024)(128)(2,1)S(1)} %dynamic-update-slice.1), channel_id=1, replica_groups=mesh['dp'=4,'expert'=8] {'dp','expert'}, use_global_device_ids=true, to_apply=%add | all-reduce | flops 2048 | bytes 8192
  108.5 5.5 convolution_convert_fusion
  121.4 4.7 convolution_convert_fusion.1
  154.4 15.8 %all-to-all-done.3 = bf16[8,36,1024]{2,1,0:T(8,128)(2,1)S(1)} async-done(((bf16[8,36,1024]{2,1,0:T(8,128)(2,1)}), bf16[8,36,1024]{2,1,0:T(8,128)(2,1)S(1)}, u32[]{:S(2)}, u32[]{:S(2)}) %all-to-all-start.3) | async-done | bytes 589856 | tf_op jit(solution)/shard_map/all_to_all | solution.py:107
  173.9 13.9 %all-gather.7.cloned.1.call-done = bf16[1,1024,4096]{2,1,0:T(8,128)(2,1)} async-done(((bf16[1,256,4096]{2,1,0:T(8,128)(2,1)}), bf16[1,1024,4096]{2,1,0:T(8,128)(2,1)}) %all-gather.7.cloned.1.call-update) | async-done | bytes 8388624 | tf_op jit(solution)/shard_map/all_gather | solution.py:44
  187.8 7.6 fusion.14
  195.3 81.8 %all-gather.9.cloned.1.call-done = bf16[1,4096,1024]{2,1,0:T(8,128)(2,1)} async-done(((bf16[1,1024,1024]{2,1,0:T(8,128)(2,1)}), bf16[1,4096,1024]{2,1,0:T(8,128)(2,1)}) %all-gather.9.cloned.1.call-update) | async-done | bytes 8388624 | tf_op jit(solution)/shard_map/all_gather | solution.py:45
  277.1 7.8 fusion.49
  286.0 4.6 all-to-all-start.4
  290.7 5.0 fusion.16
  297.8 6.5 fusion.46
  312.3 47.4 %all-gather = bf16[32,32,8]{1,2,0:T(8,128)(2,1)S(1)} all-gather(bf16[1,32,8]{1,2,0:T(8,128)(2,1)S(1)} %bitcast.297), channel_id=1, replica_groups=mesh['dp'=4,'expert'=8] {'dp','expert'}, dimensions={0}, use_global_device_ids=true | all-gather | bytes 16896 | tf_op jit(solution)/shard_map/all_gather | solution.py:36
  375.4 15.3 %all-to-all-done.5 = bf16[8,36,1024]{2,1,0:T(8,128)(2,1)S(1)} async-done(((bf16[8,36,1024]{2,1,0:T(8,128)(2,1)}), bf16[8,36,1024]{2,1,0:T(8,128)(2,1)S(1)}, u32[]{:S(2)}, u32[]{:S(2)}) %all-to-all-start.5) | async-done | bytes 589856 | tf_op jit(solution)/shard_map/all_to_all | solution.py:174
  395.9 11.2 %fusion.177 = f32[4096,1024]{1,0:T(8,128)} fusion(bf16[288,1024]{1,0:T(8,128)(2,1)S(1)} %reshape.417, f32[288,4096]{1,0:T(8,128)} %copy-done.16), kind=kOutput, calls=%fused_computation.253 | convolution fusion | flops 2426535936 | bytes 22085632 | tf_op jit(solution)/shard_map/rf,rd->fd/dot_general | solution.py:178
  407.1 5.5 all-to-all-done.7
  412.8 12.4 %fusion.1 = bf16[1,4096,1024]{2,1,0:T(8,128)(2,1)} fusion(f32[4096,1024]{1,0:T(8,128)} %fusion.177, bf16[288,1024]{1,0:T(8,128)(2,1)S(1)} %reshape.425, f32[288,4096]{1,0:T(8,128)} %fusion.14), kind=kOutput, calls=%fused_computation.3 | convolution fusion | flops 2434924544 | bytes 30474240 | tf_op jit(solution)/shard_map/rf,rd->fd/dot_general | solution.py:178
  425.5 11.6 %fusion.24 = bf16[288,4096]{1,0:T(8,128)(2,1)S(1)} fusion(f32[288,4096]{1,0:T(8,128)} %copy-done.16, bf16[288,1024]{1,0:T(8,128)(2,1)S(1)} %reshape.417, bf16[1,4096,1024]{2,1,0:T(8,128)(2,1)} %all-gather.9.cloned.1.call-done), kind=kOutput, calls=%fused_computation.31 | convolution fusion | flops 2439512064 | bytes 16056320 | tf_op jit(solution)/shard_map/rd,fd->rf/dot_general | solution.py:177
  437.1 8.2 fusion.186
  445.3 11.6 %fusion.31 = bf16[288,4096]{1,0:T(8,128)(2,1)S(1)} fusion(f32[288,4096]{1,0:T(8,128)} %fusion.14, bf16[288,1024]{1,0:T(8,128)(2,1)S(1)} %reshape.425, bf16[1,4096,1024]{2,1,0:T(8,128)(2,1)} %all-gather.9.cloned.1.call-done), kind=kOutput, calls=%fused_computation.38 | convolution fusion | flops 2439512064 | bytes 16056320 | tf_op jit(solution)/shard_map/rd,fd->rf/dot_general | solution.py:177
  458.3 10.6 %fusion = bf16[1,1024,4096]{2,1,0:T(8,128)(2,1)} fusion(f32[1024,4096]{1,0:T(8,128)} %fusion.186, bf16[288,1024]{1,0:T(8,128)(2,1)S(1)} %copy-done.46, bf16[288,4096]{1,0:T(8,128)(2,1)S(1)} %fusion.31), kind=kOutput, calls=%fused_computation.2 | convolution fusion | flops 2424307712 | bytes 28114944 | tf_op jit(solution)/shard_map/rd,rf->df/dot_general | solution.py:181
  470.6 6.0 fusion.40
  481.1 6.7 fusion.43
  488.8 11.1 %all-to-all-done.6 = bf16[8,36,1024]{2,1,0:T(8,128)(2,1)S(1)} async-done(((bf16[8,36,1024]{2,1,0:T(8,128)(2,1)}), bf16[8,36,1024]{2,1,0:T(8,128)(2,1)S(1)}, u32[]{:S(2)}, u32[]{:S(2)}) %all-to-all-start.6) | async-done | bytes 589856 | tf_op jit(solution)/shard_map/all_to_all | solution.py:184
  505.2 17.7 %all-to-all-done.8 = bf16[8,36,1024]{2,1,0:T(8,128)(2,1)} async-done(((bf16[8,36,1024]{2,1,0:T(8,128)(2,1)}), bf16[8,36,1024]{2,1,0:T(8,128)(2,1)}, u32[]{:S(2)}, u32[]{:S(2)}) %all-to-all-start.8) | async-done | bytes 589856 | tf_op jit(solution)/shard_map/all_to_all | solution.py:184
  559.9 6.8 convolution_add_fusion
  568.2 5.1 fusion.90
  573.4 6.8 fusion.84
  580.2 37.8 %all-reduce.4 = (f32[1024]{0:T(1024)S(1)}, f32[1024]{0:T(1024)S(1)}) all-reduce(f32[1024]{0:T(1024)S(1)} %add.172, f32[1024]{0:T(1024)S(1)} %add.173), channel_id=5, replica_groups=mesh['dp'=4,'expert'=8] {'dp','expert'}, use_global_device_ids=true, to_apply=%region_43.44.clone | all-reduce | flops 2048 | bytes 16384
  629.3 80.8 %reduce-scatter.12.cloned.1.call-done = bf16[1,256,4096]{2,1,0:T(8,128)(2,1)} async-done(((bf16[1,1024,4096]{2,1,0:T(8,128)(2,1)}), bf16[1,256,4096]{2,1,0:T(8,128)(2,1)}) %reduce-scatter.12.cloned.1.call-update) | async-done | bytes 2097168 | tf_op jit(solution)/shard_map/reduce_scatter | solution.py:308
  714.2 142.6 %reduce-scatter.10.cloned.1.call-done = f32[32,1024]{1,0:T(8,128)} async-done(((f32[1024,1024]{1,0:T(8,128)}), f32[32,1024]{1,0:T(8,128)}) %reduce-scatter.10.cloned.1.call-update) | async-done | bytes 131088 | tf_op jit(solution)/shard_map/reduce_scatter | solution.py:302
  856.8 158.5 %reduce-scatter.8.cloned.1.call-done = f32[32,3072]{1,0:T(8,128)} async-done(((f32[1024,3072]{1,0:T(8,128)}), f32[32,3072]{1,0:T(8,128)}) %reduce-scatter.8.cloned.1.call-update) | async-done | bytes 393232 | tf_op jit(solution)/shard_map/reduce_scatter | solution.py:301
  (296 shorter events, 144.7 us)
Async XLA Ops:
  7.2 101.3 %all-gather.5.cloned.1.call-start = ((), (), s32[]{:S(2)}) async-start(), calls=%async_computation.14 | async-start | bytes 6488064 | tf_op jit(solution)/shard_map/all_gather | solution.py:29
  7.9 179.8 %all-gather.7.cloned.1.call-start = ((), (), s32[]{:S(2)}) async-start(), calls=%async_computation.15 | async-start | bytes 10485760 | tf_op jit(solution)/shard_map/all_gather | solution.py:44
  8.7 268.4 %all-gather.9.cloned.1.call-start = ((), (), s32[]{:S(2)}) async-start(), calls=%async_computation.16 | async-start | bytes 10485760 | tf_op jit(solution)/shard_map/all_gather | solution.py:45
  9.4 10.7 %copy-start.67 = (bf16[32]{0:T(256)(128)(2,1)S(1)}, bf16[32]{0:T(256)(128)(2,1)}, u32[]{:S(2)}) copy-start(bf16[32]{0:T(256)(128)(2,1)} %param.19) | copy-start | bytes 196
  9.5 98.7 %copy-start.65 = (s32[2,1,256]{2,1,0:T(1,128)S(1)}, s32[2,1,256]{2,1,0:T(1,128)}, u32[]{:S(2)}) copy-start(s32[2,1,256]{2,1,0:T(1,128)} %param.12) | copy-start | bytes 6148
  11.0 128.4 %all-to-all-start = ((bf16[32,32,1024]{2,1,0:T(8,128)(2,1)}), bf16[32,32,1024]{2,1,0:T(8,128)(2,1)S(1)}, u32[]{:S(2)}, u32[]{:S(2)}) async-start(bf16[32,32,1024]{2,1,0:T(8,128)(2,1)} %stack.14), calls=%async_computation | async-start | bytes 4194304 | tf_op jit(solution)/shard_map/all_to_all | solution.py:31
  19.2 94.8 %copy-start.57 = (f32[256]{0:T(256)}, f32[256]{0:T(256)S(1)}, u32[]{:S(2)}) copy-start(f32[256]{0:T(256)S(1)} %get-tuple-element.104) | copy-start | bytes 3076
  19.2 102.1 %copy-start.55 = (f32[256]{0:T(256)}, f32[256]{0:T(256)S(1)}, u32[]{:S(2)}) copy-start(f32[256]{0:T(256)S(1)} %get-tuple-element.105) | copy-start | bytes 3076
  19.7 101.7 %copy-start.59 = (f32[256]{0:T(256)}, f32[256]{0:T(256)S(1)}, u32[]{:S(2)}) copy-start(f32[256]{0:T(256)S(1)} %add_rsqrt_fusion.3) | copy-start | bytes 3076
  19.7 94.3 %copy-start.61 = (f32[256]{0:T(256)}, f32[256]{0:T(256)S(1)}, u32[]{:S(2)}) copy-start(f32[256]{0:T(256)S(1)} %add_rsqrt_fusion.1) | copy-start | bytes 3076
  108.0 13.3 %copy-start.43 = (f32[1024]{0:T(1024)}, f32[1024]{0:T(1024)S(1)}, u32[]{:S(2)}) copy-start(f32[1024]{0:T(1024)S(1)} %convert_element_type.200) | copy-start | bytes 12292
  108.3 35.5 %copy-start.38 = (pred[256,256]{0,1:T(8,128)(4,1)}, pred[256,256]{0,1:T(8,128)(4,1)S(1)}, u32[]{:S(2)}) copy-start(pred[256,256]{0,1:T(8,128)(4,1)S(1)} %fusion.112) | copy-start | bytes 196612
  108.5 27.9 %copy-start.40 = (pred[256,256]{0,1:T(8,128)(4,1)}, pred[256,256]{0,1:T(8,128)(4,1)S(1)}, u32[]{:S(2)}) copy-start(pred[256,256]{0,1:T(8,128)(4,1)S(1)} %fusion.113) | copy-start | bytes 196612
  148.4 21.8 %all-to-all-start.3 = ((bf16[8,36,1024]{2,1,0:T(8,128)(2,1)}), bf16[8,36,1024]{2,1,0:T(8,128)(2,1)S(1)}, u32[]{:S(2)}, u32[]{:S(2)}) async-start(bf16[8,36,1024]{2,1,0:T(8,128)(2,1)} %reshape.412), calls=%async_computation.3 | async-start | bytes 1310720 | tf_op jit(solution)/shard_map/all_to_all | solution.py:107
  170.2 115.8 %all-to-all-start.1 = ((bf16[8,36,1024]{2,1,0:T(8,128)(2,1)}), bf16[8,36,1024]{2,1,0:T(8,128)(2,1)S(1)}, u32[]{:S(2)}, u32[]{:S(2)}) async-start(bf16[8,36,1024]{2,1,0:T(8,128)(2,1)} %reshape.404), calls=%async_computation.1 | async-start | bytes 1310720 | tf_op jit(solution)/shard_map/all_to_all | solution.py:107
  173.9 21.4 %copy-start.45 = (bf16[288,1024]{1,0:T(8,128)(2,1)}, bf16[288,1024]{1,0:T(8,128)(2,1)S(1)}, u32[]{:S(2)}) copy-start(bf16[288,1024]{1,0:T(8,128)(2,1)S(1)} %reshape.413) | copy-start | bytes 1769476
  286.0 22.7 %all-to-all-start.4 = ((bf16[8,36,1024]{2,1,0:T(8,128)(2,1)}), bf16[8,36,1024]{2,1,0:T(8,128)(2,1)S(1)}, u32[]{:S(2)}, u32[]{:S(2)}) async-start(bf16[8,36,1024]{2,1,0:T(8,128)(2,1)} %reshape.414), calls=%async_computation.4 | async-start | bytes 1310720 | tf_op jit(solution)/shard_map/all_to_all | solution.py:114
  297.8 14.4 %copy-start.63 = (bf16[32,8]{0,1:T(8,128)(2,1)S(1)}, bf16[32,8]{0,1:T(8,128)(2,1)}, u32[]{:S(2)}) copy-start(bf16[32,8]{0,1:T(8,128)(2,1)} %param.17) | copy-start | bytes 1540
  308.7 53.9 %all-to-all-start.2 = ((bf16[8,36,1024]{2,1,0:T(8,128)(2,1)}), bf16[8,36,1024]{2,1,0:T(8,128)(2,1)S(1)}, u32[]{:S(2)}, u32[]{:S(2)}) async-start(bf16[8,36,1024]{2,1,0:T(8,128)(2,1)} %reshape.406), calls=%async_computation.2 | async-start | bytes 1310720 | tf_op jit(solution)/shard_map/all_to_all | solution.py:114
  369.1 21.6 %all-to-all-start.5 = ((bf16[8,36,1024]{2,1,0:T(8,128)(2,1)}), bf16[8,36,1024]{2,1,0:T(8,128)(2,1)S(1)}, u32[]{:S(2)}, u32[]{:S(2)}) async-start(bf16[8,36,1024]{2,1,0:T(8,128)(2,1)} %reshape.416), calls=%async_computation.5 | async-start | bytes 1310720 | tf_op jit(solution)/shard_map/all_to_all | solution.py:174
  390.7 22.0 %all-to-all-start.7 = ((bf16[8,36,1024]{2,1,0:T(8,128)(2,1)}), bf16[8,36,1024]{2,1,0:T(8,128)(2,1)S(1)}, u32[]{:S(2)}, u32[]{:S(2)}) async-start(bf16[8,36,1024]{2,1,0:T(8,128)(2,1)} %reshape.424), calls=%async_computation.7 | async-start | bytes 1310720 | tf_op jit(solution)/shard_map/all_to_all | solution.py:174
  394.2 172.5 %reduce-scatter.16.cloned.1.call-start = ((), (), s32[]{:S(2)}) async-start(), calls=%async_computation.21 | async-start | bytes 540672
  395.7 229.5 %reduce-scatter.14.cloned.1.call-start = ((), (), s32[]{:S(2)}) async-start(), calls=%async_computation.20 | async-start | bytes 10485760 | tf_op jit(solution)/shard_map/reduce_scatter | solution.py:311
  425.2 284.9 %reduce-scatter.12.cloned.1.call-start = ((), (), s32[]{:S(2)}) async-start(), calls=%async_computation.19 | async-start | bytes 10485760 | tf_op jit(solution)/shard_map/reduce_scatter | solution.py:308
  445.3 13.0 %copy-start.46 = (bf16[288,1024]{1,0:T(8,128)(2,1)S(1)}, bf16[288,1024]{1,0:T(8,128)(2,1)}, u32[]{:S(2)}) copy-start(bf16[288,1024]{1,0:T(8,128)(2,1)} %copy-done.45) | copy-start | bytes 1769476
  477.5 22.3 %all-to-all-start.6 = ((bf16[8,36,1024]{2,1,0:T(8,128)(2,1)}), bf16[8,36,1024]{2,1,0:T(8,128)(2,1)S(1)}, u32[]{:S(2)}, u32[]{:S(2)}) async-start(bf16[8,36,1024]{2,1,0:T(8,128)(2,1)} %reshape.418), calls=%async_computation.6 | async-start | bytes 1310720 | tf_op jit(solution)/shard_map/all_to_all | solution.py:184
  499.9 23.0 %all-to-all-start.8 = ((bf16[8,36,1024]{2,1,0:T(8,128)(2,1)}), bf16[8,36,1024]{2,1,0:T(8,128)(2,1)}, u32[]{:S(2)}, u32[]{:S(2)}) async-start(bf16[8,36,1024]{2,1,0:T(8,128)(2,1)} %reshape.426), calls=%async_computation.8 | async-start | bytes 1310720 | tf_op jit(solution)/shard_map/all_to_all | solution.py:184
  504.1 22.6 %copy-start.9 = (f32[256,1024]{1,0:T(8,128)S(1)}, f32[256,1024]{1,0:T(8,128)}, u32[]{:S(2)}) copy-start(f32[256,1024]{1,0:T(8,128)} %copy-done.8) | copy-start | bytes 3145732
  504.1 22.6 %copy-start.11 = (f32[256,1024]{1,0:T(8,128)S(1)}, f32[256,1024]{1,0:T(8,128)}, u32[]{:S(2)}) copy-start(f32[256,1024]{1,0:T(8,128)} %copy-done.10) | copy-start | bytes 3145732
  504.1 352.7 %reduce-scatter.10.cloned.1.call-start = ((), (), s32[]{:S(2)}) async-start(), calls=%async_computation.18 | async-start | bytes 4325376 | tf_op jit(solution)/shard_map/reduce_scatter | solution.py:302
  533.9 481.4 %reduce-scatter.8.cloned.1.call-start = ((), (), s32[]{:S(2)}) async-start(), calls=%async_computation.17 | async-start | bytes 12976128 | tf_op jit(solution)/shard_map/reduce_scatter | solution.py:301
  573.4 48.0 %copy-start.13 = (f32[256,1024]{1,0:T(8,128)S(1)}, f32[256,1024]{1,0:T(8,128)}, u32[]{:S(2)}) copy-start(f32[256,1024]{1,0:T(8,128)} %copy-done.12) | copy-start | bytes 3145732
  (54 other events, 188.1 us)
Sparse Core Ops, SparseCore 0:
  11.0 88.5 all-gather.4
  101.4 86.3 all-gather.6
  189.6 87.4 all-gather.8
  397.0 137.2 reduce-scatter.15
  537.1 83.6 reduce-scatter.13
  623.8 86.2 reduce-scatter.11
  713.0 143.7 reduce-scatter.9
  863.4 151.8 reduce-scatter.7
